TPU v7x, 32 devices: a whole 2x2x4 slice. The times are simulated.
32 devices in a mesh: dp: 16 (over z, y, x), mp: 2 (over core).
Axes of the slice: x: 2, y: 2, z: 4, core: 2. Of those that a mesh axis runs over, the one named last changes fastest.
Arguments:
- inputs: bfloat16 [32, 512, 768], P('dp'), may hold values from -6 to 6
- counts: int32 [32], P('dp'), may hold values from 16 to 128, as said below
- w_qkv: bfloat16 [768, 3, 768], P(None, None, 'mp'), may hold values from -0.21875 to 0.21875
- w_out: bfloat16 [768, 768], P('mp'), may hold values from -2 to 2
- w_up: bfloat16 [768, 3072], P(None, 'mp'), may hold values from -0.21875 to 0.21875
- w_down: bfloat16 [3072, 768], P('mp'), may hold values from -0.109375 to 0.109375
- gain_one: float32 [768], replicated, may hold values from 0.1 to 1.9
- shift_one: float32 [768], replicated, may hold values from -3 to 3
- gain_two: float32 [768], replicated, may hold values from 0.1 to 1.9
- shift_two: float32 [768], replicated, may hold values from -3 to 3
- cotangent: bfloat16 [32, 512, 768], P('dp'), may hold values from -6 to 6
Outputs:
- outputs: bfloat16 [32, 512, 768], P('dp')
- grad_inputs: float32 [32, 512, 768], P('dp')
- grad_w_qkv: float32 [768, 3, 768], P('dp', None, 'mp')
- grad_w_out: float32 [768, 768], P('mp', 'dp')
- grad_w_up: float32 [768, 3072], P('dp', 'mp')
- grad_w_down: float32 [3072, 768], P('mp', 'dp')
- grad_gain_one: float32 [768], P('dp')
- grad_shift_one: float32 [768], P('dp')
- grad_gain_two: float32 [768], P('dp')
- grad_shift_two: float32 [768], P('dp')
Inputs may be any that keep to these rules, and one draw needn't show every extreme that they name: counts[t] is the number of live query rows of table t; some table has exactly 128.
All inputs are finite; a program needn't handle non-finite values.
Results may differ from a plain program's by a relative error of at most 0.015.
The roundings to bfloat16 on the way count: a program that leaves them out, or rounds other values in their place, can miss the bound.
Values may be sent and summed in bfloat16 or wider, within the bound.
A program may use at most 128 MiB of HBM per device.

v0:
```python
from functools import partial
import math
import jax
import jax.numpy as jnp
from jax import lax
from jax.sharding import PartitionSpec as P

HD = 64
CTX = 384
EPSILON = 1e-05


def layer_norm(row_data, norm_gain, norm_shift):
    centre = jnp.mean(row_data, axis=-1, keepdims=True)
    centred = row_data - centre
    inverse = lax.rsqrt(jnp.mean(centred * centred, axis=-1, keepdims=True) + EPSILON)
    unit_rows = centred * inverse
    return (unit_rows, inverse, unit_rows * norm_gain + norm_shift)


def norm_backward(grad_norm, unit_rows, inverse, norm_gain):
    grad_unit = grad_norm * norm_gain
    grad_mean = jnp.mean(grad_unit, axis=-1, keepdims=True)
    cross_mean = jnp.mean(grad_unit * unit_rows, axis=-1, keepdims=True)
    return inverse * (grad_unit - grad_mean - unit_rows * cross_mean)


def attend_forward(query_all, key_rows, value_rows, block_rows, score_scale):
    seq_len, heads_dev, head_dim = query_all.shape
    blocks = query_all.reshape(seq_len // block_rows, block_rows, heads_dev, head_dim)

    def one_block(query_block):
        scores = (
            jnp.einsum("bhd,khd->hbk", query_block, key_rows, preferred_element_type=jnp.float32)
            * score_scale
        )
        row_peak = jnp.max(scores, axis=-1, keepdims=True)
        exp_scores = jnp.exp(scores - row_peak)
        row_total = jnp.sum(exp_scores, axis=-1, keepdims=True)
        weights = (exp_scores / row_total).astype(jnp.bfloat16)
        block_out = jnp.einsum(
            "hbk,khd->bhd", weights, value_rows, preferred_element_type=jnp.float32
        )
        return (block_out.astype(jnp.bfloat16), row_peak + jnp.log(row_total))

    heads_out, log_total = lax.map(one_block, blocks)
    return (heads_out.reshape(seq_len, heads_dev * head_dim), log_total)


def attend_backward(
    query_all, key_rows, value_rows, grad_heads, log_total, block_rows, score_scale
):
    seq_len, heads_dev, head_dim = query_all.shape
    count_blocks = seq_len // block_rows
    query_blocks = query_all.reshape(count_blocks, block_rows, heads_dev, head_dim)
    grad_blocks = grad_heads.reshape(count_blocks, block_rows, heads_dev, head_dim)

    def one_block(running, block_items):
        query_block, grad_block, lse_block = block_items
        scores = (
            jnp.einsum("bhd,khd->hbk", query_block, key_rows, preferred_element_type=jnp.float32)
            * score_scale
        )
        softmax_rows = jnp.exp(scores - lse_block)
        grad_weights = jnp.einsum(
            "bhd,khd->hbk", grad_block, value_rows, preferred_element_type=jnp.float32
        )
        row_inner = jnp.sum(softmax_rows * grad_weights, axis=-1, keepdims=True)
        grad_scores = (softmax_rows * (grad_weights - row_inner)).astype(jnp.bfloat16)
        grad_query = (
            jnp.einsum("hbk,khd->bhd", grad_scores, key_rows, preferred_element_type=jnp.float32)
            * score_scale
        ).astype(jnp.bfloat16)
        grad_key = (
            running[0]
            + jnp.einsum(
                "hbk,bhd->khd", grad_scores, query_block, preferred_element_type=jnp.float32
            )
            * score_scale
        )
        grad_value = running[1] + jnp.einsum(
            "hbk,bhd->khd",
            softmax_rows.astype(jnp.bfloat16),
            grad_block,
            preferred_element_type=jnp.float32,
        )
        return ((grad_key, grad_value), grad_query)

    empty_grad = jnp.zeros(key_rows.shape, jnp.float32)
    (grad_key, grad_value), grad_query = lax.scan(
        one_block, (empty_grad, empty_grad), (query_blocks, grad_blocks, log_total)
    )
    return (
        grad_query.reshape(seq_len, heads_dev * head_dim),
        grad_key.astype(jnp.bfloat16),
        grad_value.astype(jnp.bfloat16),
    )


def reduce_total(grads):
    return (
        lax.psum_scatter(grads[0], "dp", scatter_dimension=0, tiled=True),
        lax.psum_scatter(grads[1], "dp", scatter_dimension=1, tiled=True),
        lax.psum_scatter(grads[2], "dp", scatter_dimension=0, tiled=True),
        lax.psum_scatter(grads[3], "dp", scatter_dimension=1, tiled=True),
        lax.psum_scatter(grads[4], "dp", scatter_dimension=0, tiled=True),
        lax.psum_scatter(grads[5], "dp", scatter_dimension=0, tiled=True),
        lax.psum_scatter(grads[6], "dp", scatter_dimension=0, tiled=True),
        lax.psum_scatter(grads[7], "dp", scatter_dimension=0, tiled=True),
    )


def per_device(
    inputs, counts, w_qkv, w_out, w_up, w_down, gain_one, shift_one, gain_two, shift_two, cotangent
):
    table_count, seq_len, width = inputs.shape
    heads_dev = w_out.shape[0] // HD
    block_rows = min(512, seq_len)
    score_scale = 1.0 / math.sqrt(HD)
    positions = jnp.arange(seq_len, dtype=jnp.int32)
    results = []
    grad_list = []
    totals = None
    for table_index in range(table_count):
        row_data = inputs[table_index].astype(jnp.float32)
        live_rows = (positions < CTX + counts[table_index]).astype(jnp.float32)[:, None]
        unit_one, inverse_one, normed = layer_norm(row_data, gain_one, shift_one)
        normed = normed.astype(jnp.bfloat16)
        context = normed[:CTX]
        query_all = (
            jnp.dot(normed, w_qkv[:, 0], preferred_element_type=jnp.float32)
            .astype(jnp.bfloat16)
            .reshape(seq_len, heads_dev, HD)
        )
        key_value = jnp.einsum(
            "sd,dcn->csn", context, w_qkv[:, 1:], preferred_element_type=jnp.float32
        ).astype(jnp.bfloat16)
        key_rows = key_value[0].reshape(CTX, heads_dev, HD)
        value_rows = key_value[1].reshape(CTX, heads_dev, HD)
        heads_out, log_total = attend_forward(
            query_all, key_rows, value_rows, block_rows, score_scale
        )
        attended = lax.psum(
            jnp.dot(heads_out, w_out, preferred_element_type=jnp.float32).astype(jnp.bfloat16), "mp"
        ).astype(jnp.float32)
        resid = row_data + attended
        unit_two, inverse_two, normed_two = layer_norm(resid, gain_two, shift_two)
        normed_two = normed_two.astype(jnp.bfloat16)
        lifted = jnp.dot(normed_two, w_up, preferred_element_type=jnp.float32)
        active_full, gelu_back = jax.vjp(partial(jax.nn.gelu, approximate=False), lifted)
        active = active_full.astype(jnp.bfloat16)
        mlp_out = lax.psum(
            jnp.dot(active, w_down, preferred_element_type=jnp.float32).astype(jnp.bfloat16), "mp"
        ).astype(jnp.float32)
        results.append(((resid + mlp_out) * live_rows).astype(jnp.bfloat16))
        grad_out = cotangent[table_index].astype(jnp.float32) * live_rows
        grad_low = grad_out.astype(jnp.bfloat16)
        grad_down = jnp.einsum("sf,sd->fd", active, grad_low, preferred_element_type=jnp.float32)
        grad_active = jnp.einsum("sd,fd->sf", grad_low, w_down, preferred_element_type=jnp.float32)
        grad_lifted = gelu_back(grad_active)[0].astype(jnp.bfloat16)
        grad_up = jnp.einsum(
            "sd,sf->df", normed_two, grad_lifted, preferred_element_type=jnp.float32
        )
        grad_norm_two = lax.psum(
            jnp.einsum("sf,df->sd", grad_lifted, w_up, preferred_element_type=jnp.float32).astype(
                jnp.bfloat16
            ),
            "mp",
        ).astype(jnp.float32)
        grad_gain_two = jnp.sum(grad_norm_two * unit_two, axis=0)
        grad_shift_two = jnp.sum(grad_norm_two, axis=0)
        grad_resid = grad_out + norm_backward(grad_norm_two, unit_two, inverse_two, gain_two)
        grad_attn = grad_resid.astype(jnp.bfloat16)
        grad_wout = jnp.einsum(
            "sk,sd->kd", heads_out, grad_attn, preferred_element_type=jnp.float32
        )
        grad_heads = (
            jnp.einsum("sd,kd->sk", grad_attn, w_out, preferred_element_type=jnp.float32)
            .astype(jnp.bfloat16)
            .reshape(seq_len, heads_dev, HD)
        )
        grad_query, grad_key, grad_value = attend_backward(
            query_all, key_rows, value_rows, grad_heads, log_total, block_rows, score_scale
        )
        grad_pairs = jnp.stack(
            [grad_key.reshape(CTX, heads_dev * HD), grad_value.reshape(CTX, heads_dev * HD)]
        )
        grad_wqkv = jnp.concatenate(
            [
                jnp.einsum("sd,sn->dn", normed, grad_query, preferred_element_type=jnp.float32)[
                    :, None
                ],
                jnp.einsum("sd,csn->dcn", context, grad_pairs, preferred_element_type=jnp.float32),
            ],
            axis=1,
        )
        context_part = jnp.einsum(
            "csn,dcn->sd", grad_pairs, w_qkv[:, 1:], preferred_element_type=jnp.float32
        )
        grad_norm_part = jnp.einsum(
            "sn,dn->sd", grad_query, w_qkv[:, 0], preferred_element_type=jnp.float32
        )
        grad_norm_part = grad_norm_part + jnp.concatenate(
            [context_part, jnp.zeros((seq_len - CTX, width), jnp.float32)], axis=0
        )
        grad_norm_one = lax.psum(grad_norm_part.astype(jnp.bfloat16), "mp").astype(jnp.float32)
        grad_gain_one = jnp.sum(grad_norm_one * unit_one, axis=0)
        grad_shift_one = jnp.sum(grad_norm_one, axis=0)
        grad_list.append(grad_resid + norm_backward(grad_norm_one, unit_one, inverse_one, gain_one))
        table_grads = (
            grad_wqkv,
            grad_wout,
            grad_up,
            grad_down,
            grad_gain_one,
            grad_shift_one,
            grad_gain_two,
            grad_shift_two,
        )
        totals = table_grads if totals is None else jax.tree.map(jnp.add, totals, table_grads)
    totals = reduce_total(totals)
    return (
        jnp.stack(results),
        jnp.stack(grad_list),
        totals[0],
        totals[1],
        totals[2],
        totals[3],
        totals[4],
        totals[5],
        totals[6],
        totals[7],
    )


def solution(mesh):
    in_specs = (
        P("dp", None, None),
        P("dp"),
        P(None, None, "mp"),
        P("mp", None),
        P(None, "mp"),
        P("mp", None),
        P(),
        P(),
        P(),
        P(),
        P("dp", None, None),
    )
    out_specs = (
        P("dp", None, None),
        P("dp", None, None),
        P("dp", None, "mp"),
        P("mp", "dp"),
        P("dp", "mp"),
        P("mp", "dp"),
        P("dp"),
        P("dp"),
        P("dp"),
        P("dp"),
    )
    return jax.shard_map(
        per_device, mesh=mesh, in_specs=in_specs, out_specs=out_specs, check_vma=False
    )
```

profile of v0, /device:TPU:0, one launch (start us, length us, event | category | flops | bytes accessed | tf_op | source)
XLA Modules:
  0.0 761.9 jit_solution(2233834308572963741)
XLA Ops:
  19.3 22.0 %all-reduce.14.cloned.1.call-done = bf16[512,768]{1,0:T(8,128)(2,1)} async-done(((bf16[512,768]{1,0:T(8,128)(2,1)}), bf16[512,768]{1,0:T(8,128)(2,1)}) %all-reduce.14.cloned.1.call-update) | async-done | bytes 786448 | tf_op jit(solution)/shard_map/psum | solution.py:143
  57.0 18.3 %all-reduce.16.cloned.1.call-done = bf16[512,768]{1,0:T(8,128)(2,1)} async-done(((bf16[512,768]{1,0:T(8,128)(2,1)}), bf16[512,768]{1,0:T(8,128)(2,1)}) %all-reduce.16.cloned.1.call-update) | async-done | bytes 786448 | tf_op jit(solution)/shard_map/psum | solution.py:143
  75.3 2.6 multiply_reduce_fusion.5
  78.6 8.9 %multiply_convert_fusion.2 = (bf16[512,1536]{1,0:T(8,128)(2,1)}, f32[512,1536]{1,0:T(8,128)S(1)}, f32[512,1536]{1,0:T(8,128)S(1)}) fusion(bf16[768,1536]{1,0:T(8,128)(2,1)S(1)} %copy-done, f32[768]{0:T(1024)S(1)} %copy-done.56, f32[768]{0:T(1024)S(1)} %copy-done.55, f32[512]{0:T(512)S(1)} %add_rsqrt_fusion, f32[512]{0:T(512)S(1)} %get-tuple-element.163, ...), kind=kOutput, calls=%fused_computation.24 | convolution fusion | flops 1262223360 | bytes 11808768 | tf_op jit(solution)/shard_map/dot_general | solution.py:149
  89.7 2.3 convolution_convert_fusion
  92.1 21.4 %multiply_convert_fusion.3 = (bf16[512,1536]{1,0:T(8,128)(2,1)}, f32[512,1536]{1,0:T(8,128)S(1)}, f32[512,1536]{1,0:T(8,128)S(1)}) fusion(bf16[768,1536]{1,0:T(8,128)(2,1)S(1)} %copy-done, f32[768]{0:T(1024)S(1)} %copy-done.56, f32[768]{0:T(1024)S(1)} %copy-done.55, f32[512]{0:T(512)S(1)} %get-tuple-element.162, f32[512]{0:T(512)S(1)} %broadcast_multiply_fusion.10, ...), kind=kOutput, calls=%fused_computation.37 | convolution fusion | flops 1262223360 | bytes 11808768 | tf_op jit(solution)/shard_map/dot_general | solution.py:149
  116.8 2.3 convolution_convert_fusion.1
  120.6 4.1 convolution_convert_fusion.2
  124.7 2.3 convolution_convert_fusion.3
  127.0 14.0 %all-reduce.20.cloned.1.call-done = (bf16[512,768]{1,0:T(8,128)(2,1)}, bf16[512,768]{1,0:T(8,128)(2,1)}) async-done(((bf16[512,768]{1,0:T(8,128)(2,1)}, bf16[512,768]{1,0:T(8,128)(2,1)}), (bf16[512,768]{1,0:T(8,128)(2,1)}, bf16[512,768]{1,0:T(8,128)(2,1)})) %all-reduce.20.cloned.1.call-update) | async-done | bytes 1572880 | tf_op jit(solution)/shard_map/psum | solution.py:164
  141.0 3.7 fusion.74
  144.8 3.1 fusion.64
  170.8 2.3 convolution_bitcast_fusion
  191.3 3.2 fusion.136
  194.5 4.2 convolution_add_fusion.1
  199.3 3.4 fusion.125
  202.7 3.8 convolution_add_fusion
  208.6 3.8 fusion.75
  212.4 77.1 %all-reduce.6 = (f32[768]{0:T(1024)S(1)}, f32[768]{0:T(1024)S(1)}, f32[768]{0:T(1024)S(1)}, f32[768]{0:T(1024)S(1)}) all-reduce(f32[768]{0:T(1024)S(1)} %add.239, f32[768]{0:T(1024)S(1)} %add.240, f32[768]{0:T(1024)S(1)} %add.241, f32[768]{0:T(1024)S(1)} %add.242), channel_id=6, replica_groups=mesh['dp'=16,'mp'=2] {'dp'}, use_global_device_ids=true, to_apply=%region_36.37.clone | all-reduce | flops 3072 | bytes 24576
  291.9 3.4 fusion.60
  298.5 33.4 %reduce-scatter.7.cloned.1.call-done = f32[384,48]{0,1:T(8,128)} async-done(((f32[384,768]{0,1:T(8,128)}), f32[384,48]{0,1:T(8,128)}) %reduce-scatter.7.cloned.1.call-update) | async-done | bytes 73744 | tf_op jit(solution)/shard_map/reduce_scatter | solution.py:103
  331.9 138.1 %reduce-scatter.5.cloned.1.call-done = f32[48,3,384]{2,0,1:T(8,128)} async-done(((f32[768,3,384]{2,0,1:T(8,128)}), f32[48,3,384]{2,0,1:T(8,128)}) %reduce-scatter.5.cloned.1.call-update) | async-done | bytes 221200 | tf_op jit(solution)/shard_map/reduce_scatter | solution.py:102
  469.9 142.4 %reduce-scatter.9.cloned.1.call-done = f32[48,1536]{1,0:T(8,128)} async-done(((f32[768,1536]{1,0:T(8,128)}), f32[48,1536]{1,0:T(8,128)}) %reduce-scatter.9.cloned.1.call-update) | async-done | bytes 294928 | tf_op jit(solution)/shard_map/reduce_scatter | solution.py:104
  612.3 142.3 %reduce-scatter.11.cloned.1.call-done = f32[1536,48]{0,1:T(8,128)} async-done(((f32[1536,768]{0,1:T(8,128)}), f32[1536,48]{0,1:T(8,128)}) %reduce-scatter.11.cloned.1.call-update) | async-done | bytes 294928 | tf_op jit(solution)/shard_map/reduce_scatter | solution.py:105
  (285 shorter events, 81.7 us)
Async XLA Ops:
  7.2 71.2 %copy-start = (bf16[768,1536]{1,0:T(8,128)(2,1)S(1)}, bf16[768,1536]{1,0:T(8,128)(2,1)}, u32[]{:S(2)}) copy-start(bf16[768,1536]{1,0:T(8,128)(2,1)} %param.15) | copy-start | bytes 7077892
  7.2 34.1 %all-reduce.14.cloned.1.call-start = ((), (), s32[]{:S(2)}) async-start(), calls=%async_computation.4 | async-start | bytes 1572864 | tf_op jit(solution)/shard_map/psum | solution.py:143
  19.2 56.0 %all-reduce.16.cloned.1.call-start = ((), (), s32[]{:S(2)}) async-start(), calls=%async_computation.5 | async-start | bytes 1572864 | tf_op jit(solution)/shard_map/psum | solution.py:143
  19.3 26.0 %copy-start.61 = (f32[512]{0:T(512)}, f32[512]{0:T(512)S(1)}, u32[]{:S(2)}) copy-start(f32[512]{0:T(512)S(1)} %broadcast_multiply_fusion.9) | copy-start | bytes 6148
  54.7 86.3 %all-reduce.20.cloned.1.call-start = ((), (), s32[]{:S(2)}) async-start(), calls=%async_computation.11 | async-start | bytes 3145728 | tf_op jit(solution)/shard_map/psum | solution.py:164
  56.9 87.8 %copy-start.70 = (f32[512]{0:T(512)}, f32[512]{0:T(512)S(1)}, u32[]{:S(2)}) copy-start(f32[512]{0:T(512)S(1)} %get-tuple-element.164) | copy-start | bytes 6148
  56.9 87.8 %copy-start.72 = (f32[512]{0:T(512)}, f32[512]{0:T(512)S(1)}, u32[]{:S(2)}) copy-start(f32[512]{0:T(512)S(1)} %get-tuple-element.165) | copy-start | bytes 6148
  56.9 87.8 %copy-start.74 = (f32[512]{0:T(512)}, f32[512]{0:T(512)S(1)}, u32[]{:S(2)}) copy-start(f32[512]{0:T(512)S(1)} %broadcast_multiply_fusion.10) | copy-start | bytes 6148
  77.9 14.2 %copy-start.76 = (f32[512]{0:T(512)}, f32[512]{0:T(512)S(1)}, u32[]{:S(2)}) copy-start(f32[512]{0:T(512)S(1)} %get-tuple-element.162) | copy-start | bytes 6148
  78.6 66.2 %copy-start.63 = (f32[512]{0:T(512)}, f32[512]{0:T(512)S(1)}, u32[]{:S(2)}) copy-start(f32[512]{0:T(512)S(1)} %add_rsqrt_fusion) | copy-start | bytes 6148
  78.6 8.9 %copy-start.16 = (bf16[2,512,768]{2,1,0:T(8,128)(2,1)S(1)}, bf16[2,512,768]{2,1,0:T(8,128)(2,1)}, u32[]{:S(2)}) copy-start(bf16[2,512,768]{2,1,0:T(8,128)(2,1)} %param.21) | copy-start | bytes 4718596
  78.6 8.9 %copy-start.86 = (bf16[1536,768]{1,0:T(8,128)(2,1)S(1)}, bf16[1536,768]{1,0:T(8,128)(2,1)}, u32[]{:S(2)}) copy-start(bf16[1536,768]{1,0:T(8,128)(2,1)} %param.16) | copy-start | bytes 7077892
  119.2 89.4 %all-reduce.18.cloned.1.call-start = ((), (), s32[]{:S(2)}) async-start(), calls=%async_computation.10 | async-start | bytes 6291456 | tf_op jit(solution)/shard_map/psum | solution.py:152
  124.6 16.4 %copy-start.5 = (bf16[2,512,768]{2,1,0:T(8,128)(2,1)S(1)}, bf16[2,512,768]{2,1,0:T(8,128)(2,1)}, u32[]{:S(2)}) copy-start(bf16[2,512,768]{2,1,0:T(8,128)(2,1)} %param.11) | copy-start | bytes 4718596
  124.6 16.4 %copy-start.13 = (bf16[512,768]{1,0:T(8,128)(2,1)S(1)}, bf16[512,768]{1,0:T(8,128)(2,1)}, u32[]{:S(2)}) copy-start(bf16[512,768]{1,0:T(8,128)(2,1)} %all-reduce.14.cloned.1.call-done) | copy-start | bytes 2359300
  124.6 16.4 %copy-start.77 = (f32[512]{0:T(512)S(1)}, f32[512]{0:T(512)}, u32[]{:S(2)}) copy-start(f32[512]{0:T(512)} %copy-done.76) | copy-start | bytes 6148
  141.0 8.1 %slice-start.2 = ((s8[4718592]{0:T(1024)(128)(4,1)}), s8[4194304]{0:T(1024)(128)(4,1)S(1)}, s32[]{:S(2)}) async-start(s8[4718592]{0:T(1024)(128)(4,1)} %bitcast.232), calls=%async_computation.14 | async-start | bytes 8388608
  147.9 8.4 %copy-start.9 = (f32[512,768]{1,0:T(8,128)}, f32[512,768]{1,0:T(8,128)S(1)}, u32[]{:S(2)}) copy-start(f32[512,768]{1,0:T(8,128)S(1)} %get-tuple-element.140) | copy-start | bytes 4718596
  165.2 9.6 %copy-start.42 = (bf16[1,384,384]{2,1,0:T(8,128)(2,1)}, bf16[1,384,384]{2,1,0:T(8,128)(2,1)S(1)}, u32[]{:S(2)}) copy-start(bf16[1,384,384]{2,1,0:T(8,128)(2,1)S(1)} %copy.45) | copy-start | bytes 884740
  177.2 154.6 %reduce-scatter.7.cloned.1.call-start = ((), (), s32[]{:S(2)}) async-start(), calls=%async_computation.7 | async-start | bytes 1253376 | tf_op jit(solution)/shard_map/reduce_scatter | solution.py:103
  182.1 287.8 %reduce-scatter.5.cloned.1.call-start = ((), (), s32[]{:S(2)}) async-start(), calls=%async_computation.6 | async-start | bytes 3760128 | tf_op jit(solution)/shard_map/reduce_scatter | solution.py:102
  190.7 421.7 %reduce-scatter.9.cloned.1.call-start = ((), (), s32[]{:S(2)}) async-start(), calls=%async_computation.8 | async-start | bytes 5013504 | tf_op jit(solution)/shard_map/reduce_scatter | solution.py:104
  198.7 555.9 %reduce-scatter.11.cloned.1.call-start = ((), (), s32[]{:S(2)}) async-start(), calls=%async_computation.9 | async-start | bytes 5013504 | tf_op jit(solution)/shard_map/reduce_scatter | solution.py:105
  296.6 458.0 %copy-start.1 = (bf16[768,1536]{1,0:T(8,128)(2,1)S(1)}, bf16[768,1536]{1,0:T(8,128)(2,1)}, u32[]{:S(2)}) copy-start(bf16[768,1536]{1,0:T(8,128)(2,1)} %param.15) | copy-start | bytes 7077892
  (78 other events, 154.2 us)
Sparse Core Ops, SparseCore 0:
  19.3 21.8 all-reduce.13
  54.8 20.3 all-reduce.15
  119.3 21.6 all-reduce.19
  177.4 24.5 all-reduce.17
  207.1 124.6 reduce-scatter.6
  337.4 132.4 reduce-scatter.4
  475.7 136.6 reduce-scatter.8
  618.9 135.6 reduce-scatter.10
where the time goes:
time: 771 us; the launch traced here: 762 us
  waiting for transfers between devices  511 us (66%)
  matrix products  97.8 us (13%)
  blocking collectives  77.1 us (10%)
  other arithmetic  31.8 us (4%)
  local copies, waits for them, and re-layouts  26.1 us (3%)
  between operations  17.6 us (2%)
    reduce_scatter x1, waiting for transfers between devices, reduce_total(): lax.psum_scatter(grads[2], 'dp', scatter_dimension=0, tiled=True)  142 us
    reduce_scatter x1, waiting for transfers between devices, reduce_total(): lax.psum_scatter(grads[3], 'dp', scatter_dimension=1, tiled=True)  142 us
    reduce_scatter x1, waiting for transfers between devices, reduce_total(): lax.psum_scatter(grads[0], 'dp', scatter_dimension=0, tiled=True)  138 us
    unnamed x1, blocking collectives  77.1 us
    psum x2, waiting for transfers between devices, per_device(): lax.psum(jnp.dot(heads_out, w_out, preferred_element_type=jnp.float32).as...  40.3 us
    reduce_scatter x1, waiting for transfers between devices, reduce_total(): lax.psum_scatter(grads[1], 'dp', scatter_dimension=1, tiled=True)  33.4 us
    dot_general x2, matrix products, per_device(): lifted = jnp.dot(normed_two, w_up, preferred_element_type=jnp.float32)  30.3 us
    unnamed x193, local copies, waits for them, and re-layouts  18.6 us
  transfers between devices with their start and end apart: 8, of which 7 were waited for; matrix products, arithmetic and copies ran while one was open for 6% of the time, Pallas kernels for 0%

commit v1 on v0

--- a/solution.py
+++ b/solution.py
@@ -1,3 +1,4 @@
+import functools
 from functools import partial
 import math
 import jax
@@ -8,6 +9,14 @@
 HD = 64
 CTX = 384
 EPSILON = 1e-05
+
+
+def view_gates_on_mesh(local_values, a_name):
+    v_now = jnp.sum(jax.lax.all_gather(local_values, a_name), axis=0)
+    return v_now
+
+
+_resolve_side = functools.partial(view_gates_on_mesh, a_name="mp")
 
 
 def layer_norm(row_data, norm_gain, norm_shift):
@@ -140,8 +149,8 @@
         heads_out, log_total = attend_forward(
             query_all, key_rows, value_rows, block_rows, score_scale
         )
-        attended = lax.psum(
-            jnp.dot(heads_out, w_out, preferred_element_type=jnp.float32).astype(jnp.bfloat16), "mp"
+        attended = _resolve_side(
+            jnp.dot(heads_out, w_out, preferred_element_type=jnp.float32).astype(jnp.bfloat16)
         ).astype(jnp.float32)
         resid = row_data + attended
         unit_two, inverse_two, normed_two = layer_norm(resid, gain_two, shift_two)

time: 771 us -> 744 us (0.965)
  waiting for transfers between devices: 511 us -> 491 us
  matrix products: 97.8 us -> 85.6 us
    psum x2 -> x0, waiting for transfers between devices: 40.3 us -> none  [per_device(): lax.psum(jnp.dot(heads_out, w_out, preferred_element_type=jnp.float32).as...]
    all_gather x0 -> x2, waiting for transfers between devices: none -> 21.5 us  [view_gates_on_mesh(): v_now = jnp.sum(jax.lax.all_gather(local_values, a_name), axis=0)]
    dot_general x2, matrix products: 30.3 us -> 18.2 us  [per_device(): lifted = jnp.dot(normed_two, w_up, preferred_element_type=jnp.float32)]
    unnamed x193 -> x195, local copies, waits for them, and re-layouts: 18.6 us -> 18.6 us
where the time goes in v1:
time: 744 us; the launch traced here: 735 us
  waiting for transfers between devices  491 us (66%)
  matrix products  85.6 us (12%)
  blocking collectives  77.2 us (10%)
  other arithmetic  35.8 us (5%)
  local copies, waits for them, and re-layouts  26.2 us (4%)
  between operations  17.7 us (2%)
    reduce_scatter x1, waiting for transfers between devices, reduce_total(): lax.psum_scatter(grads[3], 'dp', scatter_dimension=1, tiled=True)  143 us
    reduce_scatter x1, waiting for transfers between devices, reduce_total(): lax.psum_scatter(grads[2], 'dp', scatter_dimension=0, tiled=True)  141 us
    reduce_scatter x1, waiting for transfers between devices, reduce_total(): lax.psum_scatter(grads[0], 'dp', scatter_dimension=0, tiled=True)  138 us
    unnamed x1, blocking collectives  77.2 us
    reduce_scatter x1, waiting for transfers between devices, reduce_total(): lax.psum_scatter(grads[1], 'dp', scatter_dimension=1, tiled=True)  33.4 us
    all_gather x2, waiting for transfers between devices, view_gates_on_mesh(): v_now = jnp.sum(jax.lax.all_gather(local_values, a_name), axis=0)  21.5 us
    unnamed x195, local copies, waits for them, and re-layouts  18.6 us
    dot_general x2, matrix products, per_device(): lifted = jnp.dot(normed_two, w_up, preferred_element_type=jnp.float32)  18.2 us
  transfers between devices with their start and end apart: 8, of which 7 were waited for; matrix products, arithmetic and copies ran while one was open for 6% of the time, Pallas kernels for 0%

profile of v1, /device:TPU:0, one launch (start us, length us, event | category | flops | bytes accessed | tf_op | source)
XLA Modules:
  0.0 734.7 jit_solution(8688780927319872694)
XLA Ops:
  19.3 12.6 %all-gather.5.cloned.1.call-done = bf16[1024,768]{1,0:T(8,128)(2,1)} async-done(((bf16[512,768]{1,0:T(8,128)(2,1)}), bf16[1024,768]{1,0:T(8,128)(2,1)}) %all-gather.5.cloned.1.call-update) | async-done | bytes 1572880 | tf_op jit(solution)/shard_map/all_gather | solution.py:15
  49.6 8.9 %all-gather.7.cloned.1.call-done = bf16[1024,768]{1,0:T(8,128)(2,1)} async-done(((bf16[512,768]{1,0:T(8,128)(2,1)}), bf16[1024,768]{1,0:T(8,128)(2,1)}) %all-gather.7.cloned.1.call-update) | async-done | bytes 1572880 | tf_op jit(solution)/shard_map/all_gather | solution.py:15
  60.7 2.3 multiply_reduce_fusion.5
  63.7 8.9 %multiply_convert_fusion.2 = (bf16[512,1536]{1,0:T(8,128)(2,1)}, f32[512,1536]{1,0:T(8,128)S(1)}, f32[512,1536]{1,0:T(8,128)S(1)}) fusion(bf16[768,1536]{1,0:T(8,128)(2,1)S(1)} %copy-done, f32[768]{0:T(1024)S(1)} %copy-done.57, f32[768]{0:T(1024)S(1)} %copy-done.56, f32[512]{0:T(512)S(1)} %add_rsqrt_fusion, f32[512]{0:T(512)S(1)} %get-tuple-element.163, ...), kind=kOutput, calls=%fused_computation.24 | convolution fusion | flops 1262223360 | bytes 11808768 | tf_op jit(solution)/shard_map/dot_general | solution.py:158
  74.9 2.3 convolution_convert_fusion
  77.2 9.3 %multiply_convert_fusion.3 = (bf16[512,1536]{1,0:T(8,128)(2,1)}, f32[512,1536]{1,0:T(8,128)S(1)}, f32[512,1536]{1,0:T(8,128)S(1)}) fusion(bf16[768,1536]{1,0:T(8,128)(2,1)S(1)} %copy-done, f32[768]{0:T(1024)S(1)} %copy-done.57, f32[768]{0:T(1024)S(1)} %copy-done.56, f32[512]{0:T(512)S(1)} %get-tuple-element.162, f32[512]{0:T(512)S(1)} %broadcast_multiply_fusion.10, ...), kind=kOutput, calls=%fused_computation.37 | convolution fusion | flops 1262223360 | bytes 11808768 | tf_op jit(solution)/shard_map/dot_general | solution.py:158
  89.8 2.3 convolution_convert_fusion.1
  93.6 4.1 convolution_convert_fusion.2
  97.7 2.3 convolution_convert_fusion.3
  100.0 14.0 %all-reduce.14.cloned.1.call-done = (bf16[512,768]{1,0:T(8,128)(2,1)}, bf16[512,768]{1,0:T(8,128)(2,1)}) async-done(((bf16[512,768]{1,0:T(8,128)(2,1)}, bf16[512,768]{1,0:T(8,128)(2,1)}), (bf16[512,768]{1,0:T(8,128)(2,1)}, bf16[512,768]{1,0:T(8,128)(2,1)})) %all-reduce.14.cloned.1.call-update) | async-done | bytes 1572880 | tf_op jit(solution)/shard_map/psum | solution.py:173
  114.0 3.7 fusion.74
  117.8 3.3 fusion.64
  144.0 2.3 convolution_bitcast_fusion
  164.5 3.2 fusion.136
  167.7 4.2 convolution_add_fusion.1
  172.5 3.4 fusion.125
  175.9 3.8 convolution_add_fusion
  181.8 3.8 fusion.75
  185.6 77.2 %all-reduce.6 = (f32[768]{0:T(1024)S(1)}, f32[768]{0:T(1024)S(1)}, f32[768]{0:T(1024)S(1)}, f32[768]{0:T(1024)S(1)}) all-reduce(f32[768]{0:T(1024)S(1)} %add.235, f32[768]{0:T(1024)S(1)} %add.236, f32[768]{0:T(1024)S(1)} %add.237, f32[768]{0:T(1024)S(1)} %add.238), channel_id=8, replica_groups=mesh['dp'=16,'mp'=2] {'dp'}, use_global_device_ids=true, to_apply=%region_36.37.clone | all-reduce | flops 3072 | bytes 24576
  265.1 3.4 fusion.60
  271.7 33.4 %reduce-scatter.7.cloned.1.call-done = f32[384,48]{0,1:T(8,128)} async-done(((f32[384,768]{0,1:T(8,128)}), f32[384,48]{0,1:T(8,128)}) %reduce-scatter.7.cloned.1.call-update) | async-done | bytes 73744 | tf_op jit(solution)/shard_map/reduce_scatter | solution.py:112
  305.1 138.3 %reduce-scatter.5.cloned.1.call-done = f32[48,3,384]{2,0,1:T(8,128)} async-done(((f32[768,3,384]{2,0,1:T(8,128)}), f32[48,3,384]{2,0,1:T(8,128)}) %reduce-scatter.5.cloned.1.call-update) | async-done | bytes 221200 | tf_op jit(solution)/shard_map/reduce_scatter | solution.py:111
  443.4 141.5 %reduce-scatter.9.cloned.1.call-done = f32[48,1536]{1,0:T(8,128)} async-done(((f32[768,1536]{1,0:T(8,128)}), f32[48,1536]{1,0:T(8,128)}) %reduce-scatter.9.cloned.1.call-update) | async-done | bytes 294928 | tf_op jit(solution)/shard_map/reduce_scatter | solution.py:113
  584.8 142.7 %reduce-scatter.11.cloned.1.call-done = f32[1536,48]{0,1:T(8,128)} async-done(((f32[1536,768]{0,1:T(8,128)}), f32[1536,48]{0,1:T(8,128)}) %reduce-scatter.11.cloned.1.call-update) | async-done | bytes 294928 | tf_op jit(solution)/shard_map/reduce_scatter | solution.py:114
  (290 shorter events, 85.9 us)
Async XLA Ops:
  7.2 56.3 %copy-start = (bf16[768,1536]{1,0:T(8,128)(2,1)S(1)}, bf16[768,1536]{1,0:T(8,128)(2,1)}, u32[]{:S(2)}) copy-start(bf16[768,1536]{1,0:T(8,128)(2,1)} %param.15) | copy-start | bytes 7077892
  7.2 24.7 %all-gather.5.cloned.1.call-start = ((), (), s32[]{:S(2)}) async-start(), calls=%async_computation.8 | async-start | bytes 2359296 | tf_op jit(solution)/shard_map/all_gather | solution.py:15
  19.2 39.3 %all-gather.7.cloned.1.call-start = ((), (), s32[]{:S(2)}) async-start(), calls=%async_computation.9 | async-start | bytes 2359296 | tf_op jit(solution)/shard_map/all_gather | solution.py:15
  19.3 18.7 %copy-start.62 = (f32[512]{0:T(512)}, f32[512]{0:T(512)S(1)}, u32[]{:S(2)}) copy-start(f32[512]{0:T(512)S(1)} %broadcast_multiply_fusion.9) | copy-start | bytes 6148
  47.4 66.6 %all-reduce.14.cloned.1.call-start = ((), (), s32[]{:S(2)}) async-start(), calls=%async_computation.11 | async-start | bytes 3145728 | tf_op jit(solution)/shard_map/psum | solution.py:173
  49.6 68.2 %copy-start.71 = (f32[512]{0:T(512)}, f32[512]{0:T(512)S(1)}, u32[]{:S(2)}) copy-start(f32[512]{0:T(512)S(1)} %fusion.143) | copy-start | bytes 6148
  49.6 68.1 %copy-start.73 = (f32[512]{0:T(512)}, f32[512]{0:T(512)S(1)}, u32[]{:S(2)}) copy-start(f32[512]{0:T(512)S(1)} %fusion.144) | copy-start | bytes 6148
  49.6 68.1 %copy-start.75 = (f32[512]{0:T(512)}, f32[512]{0:T(512)S(1)}, u32[]{:S(2)}) copy-start(f32[512]{0:T(512)S(1)} %broadcast_multiply_fusion.10) | copy-start | bytes 6148
  63.0 14.1 %copy-start.77 = (f32[512]{0:T(512)}, f32[512]{0:T(512)S(1)}, u32[]{:S(2)}) copy-start(f32[512]{0:T(512)S(1)} %get-tuple-element.162) | copy-start | bytes 6148
  63.7 54.1 %copy-start.64 = (f32[512]{0:T(512)}, f32[512]{0:T(512)S(1)}, u32[]{:S(2)}) copy-start(f32[512]{0:T(512)S(1)} %add_rsqrt_fusion) | copy-start | bytes 6148
  63.7 8.9 %copy-start.17 = (bf16[2,512,768]{2,1,0:T(8,128)(2,1)S(1)}, bf16[2,512,768]{2,1,0:T(8,128)(2,1)}, u32[]{:S(2)}) copy-start(bf16[2,512,768]{2,1,0:T(8,128)(2,1)} %param.21) | copy-start | bytes 4718596
  63.7 8.9 %copy-start.87 = (bf16[1536,768]{1,0:T(8,128)(2,1)S(1)}, bf16[1536,768]{1,0:T(8,128)(2,1)}, u32[]{:S(2)}) copy-start(bf16[1536,768]{1,0:T(8,128)(2,1)} %param.16) | copy-start | bytes 7077892
  92.2 89.6 %all-reduce.12.cloned.1.call-start = ((), (), s32[]{:S(2)}) async-start(), calls=%async_computation.10 | async-start | bytes 6291456 | tf_op jit(solution)/shard_map/psum | solution.py:161
  97.6 16.3 %copy-start.5 = (bf16[2,512,768]{2,1,0:T(8,128)(2,1)S(1)}, bf16[2,512,768]{2,1,0:T(8,128)(2,1)}, u32[]{:S(2)}) copy-start(bf16[2,512,768]{2,1,0:T(8,128)(2,1)} %param.11) | copy-start | bytes 4718596
  97.6 16.3 %copy-start.10 = (bf16[512,768]{1,0:T(8,128)(2,1)S(1)}, bf16[512,768]{1,0:T(8,128)(2,1)}, u32[]{:S(2)}) copy-start(bf16[512,768]{1,0:T(8,128)(2,1)} %copy-done.8) | copy-start | bytes 2359300
  97.7 16.3 %copy-start.78 = (f32[512]{0:T(512)S(1)}, f32[512]{0:T(512)}, u32[]{:S(2)}) copy-start(f32[512]{0:T(512)} %copy-done.77) | copy-start | bytes 6148
  114.0 8.3 %slice-start.2 = ((s8[4718592]{0:T(1024)(128)(4,1)}), s8[4194304]{0:T(1024)(128)(4,1)S(1)}, s32[]{:S(2)}) async-start(s8[4718592]{0:T(1024)(128)(4,1)} %bitcast.234), calls=%async_computation.14 | async-start | bytes 8388608
  121.1 8.4 %copy-start.11 = (f32[512,768]{1,0:T(8,128)}, f32[512,768]{1,0:T(8,128)S(1)}, u32[]{:S(2)}) copy-start(f32[512,768]{1,0:T(8,128)S(1)} %get-tuple-element.140) | copy-start | bytes 4718596
  138.3 9.6 %copy-start.43 = (bf16[1,384,384]{2,1,0:T(8,128)(2,1)}, bf16[1,384,384]{2,1,0:T(8,128)(2,1)S(1)}, u32[]{:S(2)}) copy-start(bf16[1,384,384]{2,1,0:T(8,128)(2,1)S(1)} %copy.45) | copy-start | bytes 884740
  150.4 154.7 %reduce-scatter.7.cloned.1.call-start = ((), (), s32[]{:S(2)}) async-start(), calls=%async_computation.5 | async-start | bytes 1253376 | tf_op jit(solution)/shard_map/reduce_scatter | solution.py:112
  155.3 288.1 %reduce-scatter.5.cloned.1.call-start = ((), (), s32[]{:S(2)}) async-start(), calls=%async_computation.4 | async-start | bytes 3760128 | tf_op jit(solution)/shard_map/reduce_scatter | solution.py:111
  163.9 421.0 %reduce-scatter.9.cloned.1.call-start = ((), (), s32[]{:S(2)}) async-start(), calls=%async_computation.6 | async-start | bytes 5013504 | tf_op jit(solution)/shard_map/reduce_scatter | solution.py:113
  171.9 555.6 %reduce-scatter.11.cloned.1.call-start = ((), (), s32[]{:S(2)}) async-start(), calls=%async_computation.7 | async-start | bytes 5013504 | tf_op jit(solution)/shard_map/reduce_scatter | solution.py:114
  269.8 457.7 %copy-start.1 = (bf16[768,1536]{1,0:T(8,128)(2,1)S(1)}, bf16[768,1536]{1,0:T(8,128)(2,1)}, u32[]{:S(2)}) copy-start(bf16[768,1536]{1,0:T(8,128)(2,1)} %param.15) | copy-start | bytes 7077892
  (79 other events, 157.6 us)
Sparse Core Ops, SparseCore 0:
  19.3 12.4 all-gather.4
  47.5 10.9 all-gather.6
  92.3 21.6 all-reduce.13
  150.5 24.5 all-reduce.11
  180.3 124.7 reduce-scatter.6
  310.6 132.6 reduce-scatter.4
  449.1 135.6 reduce-scatter.8
  591.4 136.0 reduce-scatter.10
